TPU v7x, 128 devices: a whole 4x4x4 slice. The times are simulated.
128 devices in a mesh: dom: 16 (over z, x), band: 8 (over y, core).
Axes of the slice: x: 4, y: 4, z: 4, core: 2. Of those that a mesh axis runs over, the one named last changes fastest.
Arguments:
- orbitals: float32 [2560, 32, 8, 128], P('band', 'dom'), may hold values from -12 to 12, as said below
- potential: float32 [32, 8, 128], P('dom'), may hold values from -2 to 0
Outputs:
- filtered: float32 [2560, 32, 8, 128], P('band', 'dom')
Inputs may be any that keep to these rules, and one draw needn't show every extreme that they name: real-valued orbitals.
All inputs are finite; a program needn't handle non-finite values.
Results may differ from a plain program's by a relative error of at most 0.00029.
Values sent between devices are 32-bit elements; how exact they have to be, the bound alone decides.
A program may use at most 192 MiB of HBM per device.

v0:
```python
import jax
import jax.numpy as jnp
from jax import lax
from jax.sharding import PartitionSpec as P

PANEL = 64
PANELS = 3
NS_ITERS = 16
SHIFT = 1.0
HALF = 1.5


def with_halo(shard, sides, width):
    for axis, dim in sides:
        size, length = (lax.axis_size(axis), shard.shape[dim])
        up = [(i, (i + 1) % size) for i in range(size)]
        down = [(j, i) for i, j in up]
        last = lax.slice_in_dim(shard, length - width, length, axis=dim)
        initial = lax.slice_in_dim(shard, 0, width, axis=dim)
        before = lax.ppermute(last, axis, up)
        after = lax.ppermute(initial, axis, down)
        shard = jnp.concatenate([before, shard, after], axis=dim)
    return shard


def from_root(block, axis, source):
    block = jnp.where(lax.axis_index(axis) == source, block, jnp.zeros_like(block))
    return lax.psum(block, axis)


def hdot(left, right):
    return jnp.dot(left, right, precision=lax.Precision.HIGHEST, preferred_element_type=jnp.float32)


def rolled(values, offset, which):
    return jnp.roll(values, offset, axis=which)


def apply_h(field_pad, potential_pad):
    centre = field_pad[:, 1:-1]
    upper = field_pad[:, 2:]
    lower = field_pad[:, :-2]
    face_sum = (
        upper
        + lower
        + rolled(centre, 1, 2)
        + rolled(centre, -1, 2)
        + rolled(centre, 1, 3)
        + rolled(centre, -1, 3)
    )
    edge_sum = jnp.zeros_like(centre)
    for offset in (1, -1):
        edge_sum = (
            edge_sum
            + rolled(upper, offset, 2)
            + rolled(lower, offset, 2)
            + rolled(upper, offset, 3)
            + rolled(lower, offset, 3)
        )
        for second in (1, -1):
            edge_sum = edge_sum + rolled(rolled(centre, offset, 2), second, 3)
    laplace = (2.0 * face_sum + edge_sum - 24.0 * centre) / 6.0
    weighted = potential_pad[None] * field_pad
    middle = weighted[:, 1:-1]
    near_sum = (
        weighted[:, 2:]
        + weighted[:, :-2]
        + rolled(middle, 1, 2)
        + rolled(middle, -1, 2)
        + rolled(middle, 1, 3)
        + rolled(middle, -1, 3)
    )
    return -0.5 * laplace + 0.5 * middle + near_sum / 12.0


def inv_sqrt(correlation):
    order = correlation.shape[0]
    eye = jnp.eye(order, dtype=jnp.float32)
    scale = jnp.sqrt(jnp.sum(correlation * correlation))
    root = correlation / scale
    inverse = eye
    for turn in range(NS_ITERS):
        factor = 0.5 * (3.0 * eye - hdot(inverse, root))
        root = hdot(root, factor)
        inverse = hdot(factor, inverse)
    return inverse / jnp.sqrt(scale)


def sweep_rim(field):
    return with_halo(field, (("dom", 1),), 1)


def per_device(orbitals, potential):
    count = orbitals.shape[0]
    potential_pad = with_halo(potential, (("dom", 0),), 1)
    first = (apply_h(sweep_rim(orbitals), potential_pad) - SHIFT * orbitals) / HALF
    second = 2.0 * (apply_h(sweep_rim(first), potential_pad) - SHIFT * first) / HALF - orbitals
    shape = second.shape
    rows = second.reshape(count, -1)
    band = lax.axis_index("band")
    local_row = jnp.arange(count)
    for panel_index in range(PANELS):
        panel = rows[:PANEL]
        correlation = lax.psum(hdot(panel, panel.T), "dom")
        outgoing = hdot(inv_sqrt(correlation), panel)
        basis = from_root(outgoing, "band", panel_index)
        coeffs = lax.psum(hdot(basis, rows.T), "dom")
        keep = jnp.where((local_row < PANEL) & (band <= panel_index), 0.0, 1.0).astype(jnp.float32)
        rows = rows - keep[:, None] * hdot(coeffs.T, basis)
        rows = rows.at[:PANEL].set(jnp.where(band == panel_index, basis, rows[:PANEL]))
    return rows.reshape(shape)


def solution(mesh):
    in_specs = (P("band", "dom", None, None), P("dom", None, None))
    out_specs = P("band", "dom", None, None)
    return jax.shard_map(
        per_device, mesh=mesh, in_specs=in_specs, out_specs=out_specs, check_vma=False
    )
```

profile of v0, /device:TPU:0, one launch (start us, length us, event | category | flops | bytes accessed | tf_op | source)
XLA Modules:
  0.0 932.7 jit_solution(11688201332727117582)
XLA Ops:
  9.3 6.4 collective-permute-start
  15.8 5.5 collective-permute-start.3
  21.8 3.6 fusion.177
  25.5 4.9 fusion.11
  33.7 4.9 fusion.12
  38.6 10.7 %collective-permute-done.2 = f32[1,8,128]{2,1,0:T(8,128)S(1)} collective-permute-done((f32[1,8,128]{2,1,0:T(8,128)S(1)}, f32[1,8,128]{2,1,0:T(8,128)S(1)}, u32[]{:S(2)}, u32[]{:S(2)}) %collective-permute-start.2) | collective-permute-done | bytes 4128 | tf_op jit(solution)/shard_map/ppermute | solution.py:20
  49.9 3.4 fusion.166
  53.2 3.3 fusion.167
  62.0 3.4 fusion.172
  65.4 3.3 fusion.173
  81.4 30.6 %broadcast_multiply_fusion = (f32[320,2,8,128]{3,0,2,1:T(8,128)S(1)}, f32[320,2,8,128]{3,0,2,1:T(8,128)}) fusion(f32[320,2,8,1]{3,0,2,1:T(8,128)} %get-tuple-element.60, f32[320,2,8,127]{3,0,2,1:T(8,128)} %get-tuple-element.62, f32[320,2,8,127]{3,0,2,1:T(8,128)} %get-tuple-element.61, f32[320,2,8,1]{3,0,2,1:T(8,128)} %get-tuple-element.59, ...), kind=kLoop, calls=%fused_computation.176 | loop fusion | flops 34078720 | bytes 73400320 | tf_op jit(solution)/shard_map/div | solution.py:96
  115.8 27.6 %collective-permute-done.4 = f32[320,1,8,128]{3,0,2,1:T(8,128)} collective-permute-done((f32[320,1,8,128]{3,0,2,1:T(8,128)}, f32[320,1,8,128]{3,0,2,1:T(8,128)}, u32[]{:S(2)}, u32[]{:S(2)}) %collective-permute-start.4) | collective-permute-done | bytes 1310752 | tf_op jit(solution)/shard_map/ppermute | solution.py:21
  143.4 3.6 collective-permute-done.5
  147.0 5.8 fusion.88
  180.7 6.6 fusion.46
  187.3 9.6 %fusion.43 = (f32[320,2,8,127]{3,0,2,1:T(8,128)}, f32[320,2,8,127]{3,0,2,1:T(8,128)}, f32[320,2,8,127]{3,0,2,1:T(8,128)}, f32[320,2,8,127]{3,0,2,1:T(8,128)}, f3...) fusion(f32[320,2,8,128]{3,0,2,1:T(8,128)S(1)} %get-tuple-element.45, f32[320,1,8,128]{3,0,2,1:T(8,128)} %collective-permute-done.5, ...), kind=kLoop, calls=%fused_computation.116 | loop fusion | flops 2600960 | bytes 26091520 | tf_op jit(solution)/shard_map/concatenate | solution.py:22
  196.8 30.3 %fusion.30 = f32[320,2,8,128]{3,0,2,1:T(8,128)} fusion(f32[320,2,8,128]{3,0,2,1:T(8,128)S(1)} %get-tuple-element.45, f32[320,2,1,128]{3,0,2,1:T(8,128)S(1)} %get-tuple-element.105, f32[320,2,7,128]{3,0,2,1:T(8,128)} %copy-done.3, f32[320,2,7,128]{3,0,2,1:T(8,128)} %copy-done.4, f32[320,2,1,128]{3,0,2,1:T(8,128)S(1)} %get-tuple-element.106, ...), kind=kLoop, calls=%fused_computation.103 | loop fusion | flops 37355520 | bytes 73359360 | tf_op jit(solution)/shard_map/sub | solution.py:97
  229.1 69.7 %psum.63 = f32[64,64]{1,0:T(8,128)S(1)} all-reduce(f32[64,64]{1,0:T(8,128)S(1)} %convolution_bitcast_fusion), channel_id=1, replica_groups=mesh['dom'=16,'band'=8] {'dom'}, use_global_device_ids=true, to_apply=%region_0.1 | all-reduce | flops 4096 | bytes 32768 | tf_op jit(solution)/shard_map/psum | solution.py:104
  313.3 54.0 %all-reduce.7.cloned.1.call-done = f32[64,2048]{1,0:T(8,128)} async-done(((f32[64,2048]{1,0:T(8,128)}), f32[64,2048]{1,0:T(8,128)}) %all-reduce.7.cloned.1.call-update) | async-done | bytes 524304 | tf_op jit(solution)/shard_map/psum | solution.py:28
  367.3 4.6 fusion.52
  372.2 81.4 %all-reduce.9.cloned.1.call-done = f32[64,320]{1,0:T(8,128)} async-done(((f32[64,320]{1,0:T(8,128)}), f32[64,320]{1,0:T(8,128)}) %all-reduce.9.cloned.1.call-update) | async-done | bytes 81936 | tf_op jit(solution)/shard_map/psum | solution.py:107
  453.6 4.8 fusion.2
  459.2 72.1 %psum.66 = f32[64,64]{1,0:T(8,128)S(1)} all-reduce(f32[64,64]{1,0:T(8,128)S(1)} %fusion.211), channel_id=1, replica_groups=mesh['dom'=16,'band'=8] {'dom'}, use_global_device_ids=true, to_apply=%region_4.5 | all-reduce | flops 4096 | bytes 32768 | tf_op jit(solution)/shard_map/psum | solution.py:104
  542.0 57.1 %all-reduce.11.cloned.1.call-done = f32[64,2048]{1,0:T(8,128)} async-done(((f32[64,2048]{1,0:T(8,128)}), f32[64,2048]{1,0:T(8,128)}) %all-reduce.11.cloned.1.call-update) | async-done | bytes 524304 | tf_op jit(solution)/shard_map/psum | solution.py:28
  599.1 4.2 fusion.240
  603.3 81.6 %all-reduce.13.cloned.1.call-done = f32[64,320]{1,0:T(8,128)} async-done(((f32[64,320]{1,0:T(8,128)}), f32[64,320]{1,0:T(8,128)}) %all-reduce.13.cloned.1.call-update) | async-done | bytes 81936 | tf_op jit(solution)/shard_map/psum | solution.py:107
  685.0 4.7 fusion.1
  692.2 72.4 %psum.69 = f32[64,64]{1,0:T(8,128)S(1)} all-reduce(f32[64,64]{1,0:T(8,128)S(1)} %fusion.241), channel_id=1, replica_groups=mesh['dom'=16,'band'=8] {'dom'}, use_global_device_ids=true, to_apply=%region_8.9 | all-reduce | flops 4096 | bytes 32768 | tf_op jit(solution)/shard_map/psum | solution.py:104
  775.4 57.1 %all-reduce.15.cloned.1.call-done = f32[64,2048]{1,0:T(8,128)} async-done(((f32[64,2048]{1,0:T(8,128)}), f32[64,2048]{1,0:T(8,128)}) %all-reduce.15.cloned.1.call-update) | async-done | bytes 524304 | tf_op jit(solution)/shard_map/psum | solution.py:28
  832.5 5.0 fusion.270
  837.5 81.7 %all-reduce.17.cloned.1.call-done = f32[64,320]{1,0:T(8,128)} async-done(((f32[64,320]{1,0:T(8,128)}), f32[64,320]{1,0:T(8,128)}) %all-reduce.17.cloned.1.call-update) | async-done | bytes 81936 | tf_op jit(solution)/shard_map/psum | solution.py:107
  919.2 4.2 fusion
  (236 shorter events, 97.6 us)
Async XLA Ops:
  6.5 360.7 %all-reduce.7.cloned.1.call-start = ((), (), s32[]{:S(2)}) async-start(), calls=%async_computation | async-start | bytes 1048576 | tf_op jit(solution)/shard_map/psum | solution.py:28
  9.1 6.6 copy-start.12
  9.3 40.0 %collective-permute-start = (f32[320,1,8,128]{3,0,2,1:T(8,128)S(1)}, f32[320,1,8,128]{3,0,2,1:T(8,128)S(1)}, u32[]{:S(2)}, u32[]{:S(2)}) collective-permute-start(f32[320,1,8,128]{3,0,2,1:T(8,128)S(1)} %get-tuple-element.136), channel_id=1, source_target_pairs={{8,0},{16,8},{24,16},{32,24},{40,32},{48,40},{56,48},{64,56},{72,6... | collective-permute-start | bytes 3932168 | tf_op jit(solution)/shard_map/ppermute | solution.py:21
  15.7 33.7 %collective-permute-start.1 = (f32[320,1,8,128]{3,0,2,1:T(8,128)S(1)}, f32[320,1,8,128]{3,0,2,1:T(8,128)S(1)}, u32[]{:S(2)}, u32[]{:S(2)}) collective-permute-start(f32[320,1,8,128]{3,0,2,1:T(8,128)S(1)} %get-tuple-element.135), channel_id=1, source_target_pairs={{0,8},{8,16},{16,24},{24,32},{32,40},{40,48},{48,56},{56,64},{64,7... | collective-permute-start | bytes 3932168 | tf_op jit(solution)/shard_map/ppermute | solution.py:20
  15.7 33.6 %collective-permute-start.2 = (f32[1,8,128]{2,1,0:T(8,128)S(1)}, f32[1,8,128]{2,1,0:T(8,128)S(1)}, u32[]{:S(2)}, u32[]{:S(2)}) collective-permute-start(f32[1,8,128]{2,1,0:T(8,128)S(1)} %get-tuple-element.137), channel_id=1, source_target_pairs={{0,8},{8,16},{16,24},{24,32},{32,40},{40,48},{48,56},{56,64},{64,7... | collective-permute-start | bytes 12296 | tf_op jit(solution)/shard_map/ppermute | solution.py:20
  15.8 33.6 %collective-permute-start.3 = (f32[1,8,128]{2,1,0:T(8,128)S(1)}, f32[1,8,128]{2,1,0:T(8,128)S(1)}, u32[]{:S(2)}, u32[]{:S(2)}) collective-permute-start(f32[1,8,128]{2,1,0:T(8,128)S(1)} %get-tuple-element.138), channel_id=1, source_target_pairs={{8,0},{16,8},{24,16},{32,24},{40,32},{48,40},{56,48},{64,56},{72,6... | collective-permute-start | bytes 12296 | tf_op jit(solution)/shard_map/ppermute | solution.py:21
  21.8 11.8 %copy-start.5 = (f32[320,2,7,128]{3,0,2,1:T(8,128)}, f32[320,2,7,128]{3,0,2,1:T(8,128)S(1)}, u32[]{:S(2)}) copy-start(f32[320,2,7,128]{3,0,2,1:T(8,128)S(1)} %get-tuple-element.127) | copy-start | bytes 6881284
  21.8 11.8 %copy-start.6 = (f32[320,2,7,128]{3,0,2,1:T(8,128)}, f32[320,2,7,128]{3,0,2,1:T(8,128)S(1)}, u32[]{:S(2)}) copy-start(f32[320,2,7,128]{3,0,2,1:T(8,128)S(1)} %get-tuple-element.128) | copy-start | bytes 6881284
  59.3 1.7 copy-start.1
  61.9 18.8 %copy-start = (f32[320,3,8,128]{3,0,2,1:T(8,128)}, f32[320,3,8,128]{3,0,2,1:T(8,128)S(1)}, u32[]{:S(2)}) copy-start(f32[320,3,8,128]{3,0,2,1:T(8,128)S(1)} %get-tuple-element.130) | copy-start | bytes 11796484
  113.7 29.6 %collective-permute-start.4 = (f32[320,1,8,128]{3,0,2,1:T(8,128)}, f32[320,1,8,128]{3,0,2,1:T(8,128)}, u32[]{:S(2)}, u32[]{:S(2)}) collective-permute-start(f32[320,1,8,128]{3,0,2,1:T(8,128)} %get-tuple-element.115), channel_id=1, source_target_pairs={{8,0},{16,8},{24,16},{32,24},{40,32},{48,40},{56,48},{64,56},{72,6... | collective-permute-start | bytes 3932168 | tf_op jit(solution)/shard_map/ppermute | solution.py:21
  114.0 33.0 %collective-permute-start.5 = (f32[320,1,8,128]{3,0,2,1:T(8,128)}, f32[320,1,8,128]{3,0,2,1:T(8,128)}, u32[]{:S(2)}, u32[]{:S(2)}) collective-permute-start(f32[320,1,8,128]{3,0,2,1:T(8,128)} %get-tuple-element.116), channel_id=1, source_target_pairs={{0,8},{8,16},{16,24},{24,32},{32,40},{40,48},{48,56},{56,64},{64,7... | collective-permute-start | bytes 3932168 | tf_op jit(solution)/shard_map/ppermute | solution.py:20
  152.8 6.3 copy-start.3
  152.8 12.7 %copy-start.4 = (f32[320,2,7,128]{3,0,2,1:T(8,128)}, f32[320,2,7,128]{3,0,2,1:T(8,128)S(1)}, u32[]{:S(2)}) copy-start(f32[320,2,7,128]{3,0,2,1:T(8,128)S(1)} %get-tuple-element.102) | copy-start | bytes 6881284
  187.3 9.6 %copy-start.2 = (f32[320,2,8,128]{3,2,1,0:T(8,128)S(1)}, f32[320,2,8,128]{3,2,1,0:T(8,128)}, u32[]{:S(2)}) copy-start(f32[320,2,8,128]{3,2,1,0:T(8,128)} %param.8) | copy-start | bytes 7864324
  300.4 7.3 slice-start
  310.0 143.6 %all-reduce.9.cloned.1.call-start = ((), (), s32[]{:S(2)}) async-start(), calls=%async_computation.1 | async-start | bytes 196608 | tf_op jit(solution)/shard_map/psum | solution.py:107
  313.3 58.9 %copy-start.7 = (f32[320,2,8,128]{3,2,1,0:T(8,128)}, f32[320,2,8,128]{3,2,1,0:T(8,128)S(1)}, u32[]{:S(2)}) copy-start(f32[320,2,8,128]{3,2,1,0:T(8,128)S(1)} %copy.35) | copy-start | bytes 7864324
  367.3 86.3 %copy-start.8 = (f32[64,2048]{1,0:T(8,128)S(1)}, f32[64,2048]{1,0:T(8,128)}, u32[]{:S(2)}) copy-start(f32[64,2048]{1,0:T(8,128)} %all-reduce.7.cloned.1.call-done) | copy-start | bytes 1572868
  371.9 227.2 %all-reduce.11.cloned.1.call-start = ((), (), s32[]{:S(2)}) async-start(), calls=%async_computation.2 | async-start | bytes 1048576 | tf_op jit(solution)/shard_map/psum | solution.py:28
  453.6 4.8 copy-start.9
  542.0 143.0 %all-reduce.13.cloned.1.call-start = ((), (), s32[]{:S(2)}) async-start(), calls=%async_computation.3 | async-start | bytes 196608 | tf_op jit(solution)/shard_map/psum | solution.py:107
  599.1 85.9 %copy-start.10 = (f32[64,2048]{1,0:T(8,128)S(1)}, f32[64,2048]{1,0:T(8,128)}, u32[]{:S(2)}) copy-start(f32[64,2048]{1,0:T(8,128)} %all-reduce.11.cloned.1.call-done) | copy-start | bytes 1572868
  603.3 229.2 %all-reduce.15.cloned.1.call-start = ((), (), s32[]{:S(2)}) async-start(), calls=%async_computation.4 | async-start | bytes 1048576 | tf_op jit(solution)/shard_map/psum | solution.py:28
  775.4 143.9 %all-reduce.17.cloned.1.call-start = ((), (), s32[]{:S(2)}) async-start(), calls=%async_computation.5 | async-start | bytes 196608 | tf_op jit(solution)/shard_map/psum | solution.py:107
  832.5 86.7 %copy-start.11 = (f32[64,2048]{1,0:T(8,128)S(1)}, f32[64,2048]{1,0:T(8,128)}, u32[]{:S(2)}) copy-start(f32[64,2048]{1,0:T(8,128)} %all-reduce.15.cloned.1.call-done) | copy-start | bytes 1572868
Sparse Core Ops, SparseCore 0:
  310.1 57.1 all-reduce.6
  372.0 81.5 all-reduce.8
  542.1 56.9 all-reduce.10
  603.4 81.5 all-reduce.12
  775.5 56.9 all-reduce.14
  837.6 81.5 all-reduce.16
where the time goes:
time: 936 us; the launch traced here: 933 us
  waiting for transfers between devices  455 us (49%)
  blocking collectives  214 us (23%)
  other arithmetic  115 us (12%)
  local copies, waits for them, and re-layouts  58.9 us (6%)
  matrix products  57.9 us (6%)
  between operations  17 us (2%)
  starting transfers between devices  14.4 us (2%)
    psum x3, waiting for transfers between devices, per_device(): coeffs = lax.psum(hdot(basis, rows.T), 'dom')  245 us
    psum x3, blocking collectives, per_device(): correlation = lax.psum(hdot(panel, panel.T), 'dom')  214 us
    psum x3, waiting for transfers between devices, from_root(): return lax.psum(block, axis)  168 us
    dot_general x153, matrix products, hdot(): jnp.dot(left, right, precision=lax.Precision.HIGHEST, preferred_element_t...  57.9 us
    slice x20, local copies, waits for them, and re-layouts, rolled(): return jnp.roll(values, offset, axis=which)  46.2 us
    div x1, other arithmetic, per_device(): (apply_h(sweep_rim(orbitals), potential_pad) - SHIFT * orbitals) / HALF  30.6 us
    sub x1, other arithmetic, per_device(): 2.0 * (apply_h(sweep_rim(first), potential_pad) - SHIFT * first) / HALF  30.3 us
    ppermute x3, waiting for transfers between devices, with_halo(): after = lax.ppermute(initial, axis, down)  27.6 us
  transfers between devices with their start and end apart: 12, of which 9 were waited for; matrix products, arithmetic and copies ran while one was open for 2% of the time, Pallas kernels for 0%

commit v1 on v0

--- a/solution.py
+++ b/solution.py
@@ -101,7 +101,7 @@
     local_row = jnp.arange(count)
     for panel_index in range(PANELS):
         panel = rows[:PANEL]
-        correlation = lax.psum(hdot(panel, panel.T), "dom")
+        correlation = jnp.sum(lax.all_gather(hdot(panel, panel.T), "dom"), axis=0)
         outgoing = hdot(inv_sqrt(correlation), panel)
         basis = from_root(outgoing, "band", panel_index)
         coeffs = lax.psum(hdot(basis, rows.T), "dom")

time: 936 us -> 799 us (0.85)
  blocking collectives: 214 us -> 67.2 us
    psum x3 -> x0, blocking collectives: 214 us -> none  [per_device(): correlation = lax.psum(hdot(panel, panel.T), 'dom')]
    all_gather x0 -> x3, blocking collectives: none -> 67.2 us  [per_device(): correlation = jnp.sum(lax.all_gather(hdot(panel, panel.T), 'dom'), axis=0)]
  transfers between devices with their start and end apart: 12 -> 12, of which waited for: 9 -> 9; matrix products, arithmetic and copies ran while one was open for 2% -> 3% of each run, Pallas kernels for 0% -> 0%
where the time goes in v1:
time: 799 us; the launch traced here: 796 us
  waiting for transfers between devices  464 us (58%)
  other arithmetic  116 us (15%)
  blocking collectives  67.2 us (8%)
  local copies, waits for them, and re-layouts  58.9 us (7%)
  matrix products  57.8 us (7%)
  between operations  17.1 us (2%)
  starting transfers between devices  14.7 us (2%)
    psum x3, waiting for transfers between devices, per_device(): coeffs = lax.psum(hdot(basis, rows.T), 'dom')  244 us
    psum x3, waiting for transfers between devices, from_root(): return lax.psum(block, axis)  177 us
    all_gather x3, blocking collectives, per_device(): correlation = jnp.sum(lax.all_gather(hdot(panel, panel.T), 'dom'), axis=0)  67.2 us
    dot_general x153, matrix products, hdot(): jnp.dot(left, right, precision=lax.Precision.HIGHEST, preferred_element_t...  57.8 us
    slice x20, local copies, waits for them, and re-layouts, rolled(): return jnp.roll(values, offset, axis=which)  46.2 us
    div x1, other arithmetic, per_device(): (apply_h(sweep_rim(orbitals), potential_pad) - SHIFT * orbitals) / HALF  30.6 us
    sub x1, other arithmetic, per_device(): 2.0 * (apply_h(sweep_rim(first), potential_pad) - SHIFT * first) / HALF  30.3 us
    ppermute x3, waiting for transfers between devices, with_halo(): after = lax.ppermute(initial, axis, down)  27.6 us
  transfers between devices with their start and end apart: 12, of which 9 were waited for; matrix products, arithmetic and copies ran while one was open for 3% of the time, Pallas kernels for 0%

profile of v1, /device:TPU:0, one launch (start us, length us, event | category | flops | bytes accessed | tf_op | source)
XLA Modules:
  0.0 795.8 jit_solution(8913340451479719481)
XLA Ops:
  9.3 6.4 collective-permute-start
  15.8 5.5 collective-permute-start.3
  21.8 3.6 fusion.177
  25.5 4.9 fusion.11
  33.7 4.9 fusion.12
  38.6 10.7 %collective-permute-done.2 = f32[1,8,128]{2,1,0:T(8,128)S(1)} collective-permute-done((f32[1,8,128]{2,1,0:T(8,128)S(1)}, f32[1,8,128]{2,1,0:T(8,128)S(1)}, u32[]{:S(2)}, u32[]{:S(2)}) %collective-permute-start.2) | collective-permute-done | bytes 4128 | tf_op jit(solution)/shard_map/ppermute | solution.py:20
  49.9 3.4 fusion.166
  53.2 3.3 fusion.167
  62.0 3.4 fusion.172
  65.4 3.3 fusion.173
  81.4 30.6 %broadcast_multiply_fusion = (f32[320,2,8,128]{3,0,2,1:T(8,128)S(1)}, f32[320,2,8,128]{3,0,2,1:T(8,128)}) fusion(f32[320,2,8,1]{3,0,2,1:T(8,128)} %get-tuple-element.60, f32[320,2,8,127]{3,0,2,1:T(8,128)} %get-tuple-element.62, f32[320,2,8,127]{3,0,2,1:T(8,128)} %get-tuple-element.61, f32[320,2,8,1]{3,0,2,1:T(8,128)} %get-tuple-element.59, ...), kind=kLoop, calls=%fused_computation.176 | loop fusion | flops 34078720 | bytes 73400320 | tf_op jit(solution)/shard_map/div | solution.py:96
  115.8 27.6 %collective-permute-done.4 = f32[320,1,8,128]{3,0,2,1:T(8,128)} collective-permute-done((f32[320,1,8,128]{3,0,2,1:T(8,128)}, f32[320,1,8,128]{3,0,2,1:T(8,128)}, u32[]{:S(2)}, u32[]{:S(2)}) %collective-permute-start.4) | collective-permute-done | bytes 1310752 | tf_op jit(solution)/shard_map/ppermute | solution.py:21
  143.4 3.6 collective-permute-done.5
  147.0 5.8 fusion.88
  180.7 6.6 fusion.46
  187.3 9.6 %fusion.43 = (f32[320,2,8,127]{3,0,2,1:T(8,128)}, f32[320,2,8,127]{3,0,2,1:T(8,128)}, f32[320,2,8,127]{3,0,2,1:T(8,128)}, f32[320,2,8,127]{3,0,2,1:T(8,128)}, f3...) fusion(f32[320,2,8,128]{3,0,2,1:T(8,128)S(1)} %get-tuple-element.45, f32[320,1,8,128]{3,0,2,1:T(8,128)} %collective-permute-done.5, ...), kind=kLoop, calls=%fused_computation.116 | loop fusion | flops 2600960 | bytes 26091520 | tf_op jit(solution)/shard_map/concatenate | solution.py:22
  196.8 30.3 %fusion.30 = f32[320,2,8,128]{3,0,2,1:T(8,128)} fusion(f32[320,2,8,128]{3,0,2,1:T(8,128)S(1)} %get-tuple-element.45, f32[320,2,1,128]{3,0,2,1:T(8,128)S(1)} %get-tuple-element.105, f32[320,2,7,128]{3,0,2,1:T(8,128)} %copy-done.3, f32[320,2,7,128]{3,0,2,1:T(8,128)} %copy-done.4, f32[320,2,1,128]{3,0,2,1:T(8,128)S(1)} %get-tuple-element.106, ...), kind=kLoop, calls=%fused_computation.103 | loop fusion | flops 37355520 | bytes 73359360 | tf_op jit(solution)/shard_map/sub | solution.py:97
  229.1 20.9 %all-gather = f32[1024,64]{1,0:T(8,128)S(1)} all-gather(f32[64,64]{1,0:T(8,128)S(1)} %convolution_bitcast_fusion), channel_id=2, replica_groups=mesh['dom'=16,'band'=8] {'dom'}, dimensions={0}, use_global_device_ids=true | all-gather | bytes 278528 | tf_op jit(solution)/shard_map/all_gather | solution.py:104
  264.6 57.6 %all-reduce.7.cloned.1.call-done = f32[64,2048]{1,0:T(8,128)} async-done(((f32[64,2048]{1,0:T(8,128)}), f32[64,2048]{1,0:T(8,128)}) %all-reduce.7.cloned.1.call-update) | async-done | bytes 524304 | tf_op jit(solution)/shard_map/psum | solution.py:28
  322.2 4.6 fusion.52
  327.1 81.4 %all-reduce.9.cloned.1.call-done = f32[64,320]{1,0:T(8,128)} async-done(((f32[64,320]{1,0:T(8,128)}), f32[64,320]{1,0:T(8,128)}) %all-reduce.9.cloned.1.call-update) | async-done | bytes 81936 | tf_op jit(solution)/shard_map/psum | solution.py:107
  408.5 4.8 fusion.2
  414.1 24.2 %all-gather.1 = f32[1024,64]{1,0:T(8,128)} all-gather(f32[64,64]{1,0:T(8,128)S(1)} %fusion.211), channel_id=3, replica_groups=mesh['dom'=16,'band'=8] {'dom'}, dimensions={0}, use_global_device_ids=true | all-gather | bytes 278528 | tf_op jit(solution)/shard_map/all_gather | solution.py:104
  450.1 59.8 %all-reduce.11.cloned.1.call-done = f32[64,2048]{1,0:T(8,128)} async-done(((f32[64,2048]{1,0:T(8,128)}), f32[64,2048]{1,0:T(8,128)}) %all-reduce.11.cloned.1.call-update) | async-done | bytes 524304 | tf_op jit(solution)/shard_map/psum | solution.py:28
  509.9 4.2 fusion.240
  514.4 81.4 %all-reduce.13.cloned.1.call-done = f32[64,320]{1,0:T(8,128)} async-done(((f32[64,320]{1,0:T(8,128)}), f32[64,320]{1,0:T(8,128)}) %all-reduce.13.cloned.1.call-update) | async-done | bytes 81936 | tf_op jit(solution)/shard_map/psum | solution.py:107
  595.8 4.7 fusion.1
  603.0 22.1 %all-gather.2 = f32[1024,64]{1,0:T(8,128)S(1)} all-gather(f32[64,64]{1,0:T(8,128)S(1)} %fusion.241), channel_id=4, replica_groups=mesh['dom'=16,'band'=8] {'dom'}, dimensions={0}, use_global_device_ids=true | all-gather | bytes 278528 | tf_op jit(solution)/shard_map/all_gather | solution.py:104
  635.9 59.7 %all-reduce.15.cloned.1.call-done = f32[64,2048]{1,0:T(8,128)} async-done(((f32[64,2048]{1,0:T(8,128)}), f32[64,2048]{1,0:T(8,128)}) %all-reduce.15.cloned.1.call-update) | async-done | bytes 524304 | tf_op jit(solution)/shard_map/psum | solution.py:28
  695.7 5.0 fusion.270
  700.7 81.7 %all-reduce.17.cloned.1.call-done = f32[64,320]{1,0:T(8,128)} async-done(((f32[64,320]{1,0:T(8,128)}), f32[64,320]{1,0:T(8,128)}) %all-reduce.17.cloned.1.call-update) | async-done | bytes 81936 | tf_op jit(solution)/shard_map/psum | solution.py:107
  782.4 4.2 fusion
  (239 shorter events, 98.9 us)
Async XLA Ops:
  6.5 315.7 %all-reduce.7.cloned.1.call-start = ((), (), s32[]{:S(2)}) async-start(), calls=%async_computation | async-start | bytes 1048576 | tf_op jit(solution)/shard_map/psum | solution.py:28
  9.1 6.6 copy-start.12
  9.3 40.0 %collective-permute-start = (f32[320,1,8,128]{3,0,2,1:T(8,128)S(1)}, f32[320,1,8,128]{3,0,2,1:T(8,128)S(1)}, u32[]{:S(2)}, u32[]{:S(2)}) collective-permute-start(f32[320,1,8,128]{3,0,2,1:T(8,128)S(1)} %get-tuple-element.136), channel_id=1, source_target_pairs={{8,0},{16,8},{24,16},{32,24},{40,32},{48,40},{56,48},{64,56},{72,6... | collective-permute-start | bytes 3932168 | tf_op jit(solution)/shard_map/ppermute | solution.py:21
  15.7 33.7 %collective-permute-start.1 = (f32[320,1,8,128]{3,0,2,1:T(8,128)S(1)}, f32[320,1,8,128]{3,0,2,1:T(8,128)S(1)}, u32[]{:S(2)}, u32[]{:S(2)}) collective-permute-start(f32[320,1,8,128]{3,0,2,1:T(8,128)S(1)} %get-tuple-element.135), channel_id=1, source_target_pairs={{0,8},{8,16},{16,24},{24,32},{32,40},{40,48},{48,56},{56,64},{64,7... | collective-permute-start | bytes 3932168 | tf_op jit(solution)/shard_map/ppermute | solution.py:20
  15.7 33.6 %collective-permute-start.2 = (f32[1,8,128]{2,1,0:T(8,128)S(1)}, f32[1,8,128]{2,1,0:T(8,128)S(1)}, u32[]{:S(2)}, u32[]{:S(2)}) collective-permute-start(f32[1,8,128]{2,1,0:T(8,128)S(1)} %get-tuple-element.137), channel_id=1, source_target_pairs={{0,8},{8,16},{16,24},{24,32},{32,40},{40,48},{48,56},{56,64},{64,7... | collective-permute-start | bytes 12296 | tf_op jit(solution)/shard_map/ppermute | solution.py:20
  15.8 33.6 %collective-permute-start.3 = (f32[1,8,128]{2,1,0:T(8,128)S(1)}, f32[1,8,128]{2,1,0:T(8,128)S(1)}, u32[]{:S(2)}, u32[]{:S(2)}) collective-permute-start(f32[1,8,128]{2,1,0:T(8,128)S(1)} %get-tuple-element.138), channel_id=1, source_target_pairs={{8,0},{16,8},{24,16},{32,24},{40,32},{48,40},{56,48},{64,56},{72,6... | collective-permute-start | bytes 12296 | tf_op jit(solution)/shard_map/ppermute | solution.py:21
  21.8 11.8 %copy-start.5 = (f32[320,2,7,128]{3,0,2,1:T(8,128)}, f32[320,2,7,128]{3,0,2,1:T(8,128)S(1)}, u32[]{:S(2)}) copy-start(f32[320,2,7,128]{3,0,2,1:T(8,128)S(1)} %get-tuple-element.127) | copy-start | bytes 6881284
  21.8 11.8 %copy-start.6 = (f32[320,2,7,128]{3,0,2,1:T(8,128)}, f32[320,2,7,128]{3,0,2,1:T(8,128)S(1)}, u32[]{:S(2)}) copy-start(f32[320,2,7,128]{3,0,2,1:T(8,128)S(1)} %get-tuple-element.128) | copy-start | bytes 6881284
  59.3 1.7 copy-start.1
  61.9 18.8 %copy-start = (f32[320,3,8,128]{3,0,2,1:T(8,128)}, f32[320,3,8,128]{3,0,2,1:T(8,128)S(1)}, u32[]{:S(2)}) copy-start(f32[320,3,8,128]{3,0,2,1:T(8,128)S(1)} %get-tuple-element.130) | copy-start | bytes 11796484
  113.7 29.6 %collective-permute-start.4 = (f32[320,1,8,128]{3,0,2,1:T(8,128)}, f32[320,1,8,128]{3,0,2,1:T(8,128)}, u32[]{:S(2)}, u32[]{:S(2)}) collective-permute-start(f32[320,1,8,128]{3,0,2,1:T(8,128)} %get-tuple-element.115), channel_id=1, source_target_pairs={{8,0},{16,8},{24,16},{32,24},{40,32},{48,40},{56,48},{64,56},{72,6... | collective-permute-start | bytes 3932168 | tf_op jit(solution)/shard_map/ppermute | solution.py:21
  114.0 33.0 %collective-permute-start.5 = (f32[320,1,8,128]{3,0,2,1:T(8,128)}, f32[320,1,8,128]{3,0,2,1:T(8,128)}, u32[]{:S(2)}, u32[]{:S(2)}) collective-permute-start(f32[320,1,8,128]{3,0,2,1:T(8,128)} %get-tuple-element.116), channel_id=1, source_target_pairs={{0,8},{8,16},{16,24},{24,32},{32,40},{40,48},{48,56},{56,64},{64,7... | collective-permute-start | bytes 3932168 | tf_op jit(solution)/shard_map/ppermute | solution.py:20
  152.8 6.3 copy-start.3
  152.8 12.7 %copy-start.4 = (f32[320,2,7,128]{3,0,2,1:T(8,128)}, f32[320,2,7,128]{3,0,2,1:T(8,128)S(1)}, u32[]{:S(2)}) copy-start(f32[320,2,7,128]{3,0,2,1:T(8,128)S(1)} %get-tuple-element.102) | copy-start | bytes 6881284
  187.3 9.6 %copy-start.2 = (f32[320,2,8,128]{3,2,1,0:T(8,128)S(1)}, f32[320,2,8,128]{3,2,1,0:T(8,128)}, u32[]{:S(2)}) copy-start(f32[320,2,8,128]{3,2,1,0:T(8,128)} %param.8) | copy-start | bytes 7864324
  251.7 7.3 slice-start
  261.2 147.3 %all-reduce.9.cloned.1.call-start = ((), (), s32[]{:S(2)}) async-start(), calls=%async_computation.1 | async-start | bytes 196608 | tf_op jit(solution)/shard_map/psum | solution.py:107
  264.6 62.6 %copy-start.7 = (f32[320,2,8,128]{3,2,1,0:T(8,128)}, f32[320,2,8,128]{3,2,1,0:T(8,128)S(1)}, u32[]{:S(2)}) copy-start(f32[320,2,8,128]{3,2,1,0:T(8,128)S(1)} %copy.53) | copy-start | bytes 7864324
  322.2 86.3 %copy-start.8 = (f32[64,2048]{1,0:T(8,128)S(1)}, f32[64,2048]{1,0:T(8,128)}, u32[]{:S(2)}) copy-start(f32[64,2048]{1,0:T(8,128)} %all-reduce.7.cloned.1.call-done) | copy-start | bytes 1572868
  326.8 183.0 %all-reduce.11.cloned.1.call-start = ((), (), s32[]{:S(2)}) async-start(), calls=%async_computation.2 | async-start | bytes 1048576 | tf_op jit(solution)/shard_map/psum | solution.py:28
  408.5 4.8 copy-start.9
  450.1 145.7 %all-reduce.13.cloned.1.call-start = ((), (), s32[]{:S(2)}) async-start(), calls=%async_computation.3 | async-start | bytes 196608 | tf_op jit(solution)/shard_map/psum | solution.py:107
  509.9 85.9 %copy-start.10 = (f32[64,2048]{1,0:T(8,128)S(1)}, f32[64,2048]{1,0:T(8,128)}, u32[]{:S(2)}) copy-start(f32[64,2048]{1,0:T(8,128)} %all-reduce.11.cloned.1.call-done) | copy-start | bytes 1572868
  514.1 181.6 %all-reduce.15.cloned.1.call-start = ((), (), s32[]{:S(2)}) async-start(), calls=%async_computation.4 | async-start | bytes 1048576 | tf_op jit(solution)/shard_map/psum | solution.py:28
  635.9 146.5 %all-reduce.17.cloned.1.call-start = ((), (), s32[]{:S(2)}) async-start(), calls=%async_computation.5 | async-start | bytes 196608 | tf_op jit(solution)/shard_map/psum | solution.py:107
  695.7 86.7 %copy-start.11 = (f32[64,2048]{1,0:T(8,128)S(1)}, f32[64,2048]{1,0:T(8,128)}, u32[]{:S(2)}) copy-start(f32[64,2048]{1,0:T(8,128)} %all-reduce.15.cloned.1.call-done) | copy-start | bytes 1572868
Sparse Core Ops, SparseCore 0:
  261.4 60.8 all-reduce.6
  327.0 81.5 all-reduce.8
  450.2 59.6 all-reduce.10
  514.2 81.5 all-reduce.12
  636.0 59.6 all-reduce.14
  700.8 81.5 all-reduce.16
